TPU v7x, 256 devices: a whole 4x4x8 slice. The times are simulated.
256 devices in a mesh: tp: 8 (over y, core), ep: 32 (over z, x).
Axes of the slice: x: 4, y: 4, z: 8, core: 2. Of those that a mesh axis runs over, the one named last changes fastest.
Arguments:
- tokens: bfloat16 [512, 8192], P('ep'), may hold values from -6 to 6
- cotangent: bfloat16 [512, 8192], P('ep'), may hold values from -6 to 6
- w_gate: bfloat16 [14336, 8192], P(('tp', 'ep')), may hold values from -0.0625 to 0.0625
- w_up: bfloat16 [14336, 8192], P(('tp', 'ep')), may hold values from -0.0625 to 0.0625
- w_down: bfloat16 [14336, 8192], P(('tp', 'ep')), may hold values from -0.375 to 0.375
- neuron_expert: int32 [14336], P(('tp', 'ep')), may hold values from 0 to 63, as said below
- neuron_slot: int32 [14336], P(('tp', 'ep')), may hold values from 0 to 63, as said below
- choice_expert: int32 [512, 8], P('ep'), may hold values from 0 to 63, all different within a row; in each aligned block of 16 rows (0 to 15, 16 to 31, ...) at most 4 rows name the same one
- choice_weight: float32 [512, 8], P('ep'), may hold values from 0.02 to 0.3
Outputs:
- output: bfloat16 [512, 8192], P('ep', 'tp')
- d_tokens: bfloat16 [512, 8192], P('ep', 'tp')
- d_weight: float32 [512, 8], P('ep')
- d_gate_exp: bfloat16 [64, 512, 8192], P('ep', 'tp')
- d_up_exp: bfloat16 [64, 512, 8192], P('ep', 'tp')
- d_down_exp: bfloat16 [64, 512, 8192], P('ep', 'tp')
Inputs may be any that keep to these rules, and one draw needn't show every extreme that they name: `neuron_expert`: expert e belongs to ep index e // 2. Among the 56 neurons starting at any multiple of 56, at most 4 name experts of one ep index. `neuron_slot`: within each tp range of 1792 neurons, the neurons of one expert have distinct slots. `choice_expert`: each row names 8 different experts; in each aligned block of 16 rows no expert is named more than 4 times.
All inputs are finite; a program needn't handle non-finite values.
Results may differ from a plain program's by a relative error of at most 0.018.
Values may be sent and summed in bfloat16 or wider, within the bound.
No kernel may reach another device: no remote copies, remote signals or barrier semaphores. Data moves between devices by JAX's collectives and lax.ppermute only.
A program may use at most 128 MiB of HBM per device.

v0:
```python
import jax
import jax.numpy as jnp
from jax import lax
from jax.experimental import pallas as pl
from jax.experimental.pallas import tpu as pltpu
from jax.sharding import PartitionSpec as P


NX = 4
NZ = 8
NY = 4
PEER = 4
CAPN = 64
EXPERTS = 64
E_DEV = 2
TCAP = 128
BF = jnp.bfloat16
F32 = jnp.float32


def move_x(v, s):
    pairs = [(z * NX + x, z * NX + (x + s) % NX) for z in range(NZ) for x in range(NX)]
    return lax.ppermute(v, "ep", pairs)


def move_z(v, s):
    pairs = [(z * NX + x, (z + s) % NZ * NX + x) for z in range(NZ) for x in range(NX)]
    return lax.ppermute(v, "ep", pairs)


def move_y(v, s):
    pairs = [(y * 2 + c, (y + s) % NY * 2 + c) for y in range(NY) for c in range(2)]
    return lax.ppermute(v, "tp", pairs)


def swap_core(v):
    return lax.ppermute(v, "tp", [(i, i ^ 1) for i in range(2 * NY)])


def mm(a, b, dims):
    return lax.dot_general(a, b, (dims, ((), ())), preferred_element_type=F32)


def gather_tokens(block):
    near = jnp.stack(
        [block, move_x(block, -1), move_x(block, -2), move_x(block, 1)],
        0,
    )
    up = [near]
    down = [near]
    for _ in range(3):
        up.append(move_z(up[-1], -1))
        down.append(move_z(down[-1], 1))
    far = jnp.concatenate([move_z(up[3][:2], -1), move_z(down[3][2:], 1)], 0)
    return jnp.stack(up + [far] + down[:0:-1], 1)


def exchange_weights(w_gate, w_up, w_down, y, c):
    two = w_gate.shape[1] // NY
    one = two // 2

    def piece(s):
        start = (y + s) % NY * two
        rows = [lax.dynamic_slice_in_dim(w, start, two, 1) for w in (w_gate, w_up, w_down)]
        return jnp.concatenate(rows, 0)

    before = move_y(piece(1), 1)
    after = move_y(piece(3), -1)
    far = move_y(piece(2), 2)
    got = [piece(0), after, far, before]
    other = jnp.stack([lax.dynamic_slice_in_dim(g, (1 - c) * one, one, 1) for g in got], 0)
    mine = jnp.stack([lax.dynamic_slice_in_dim(g, c * one, one, 1) for g in got], 0)
    return mine, swap_core(other)


def gather_tp(v):
    near = jnp.stack([v] + [move_y(v, -s) for s in range(1, NY)], 0)
    return near, swap_core(near)


def reduce_tp(near, far):
    half = near + swap_core(far.astype(BF)).astype(F32)
    total = half[0]
    for s in range(1, NY):
        total = total + move_y(half[s].astype(BF), s).astype(F32)
    return total


def combine_kernel(order, near, far, w_near, w_far, own, *outs):
    nl = w_near.shape[1] // 3
    lw = w_near.shape[2]
    parts = [(near, w_near, i) for i in range(NY)] + [(far, w_far, i) for i in range(NY)]
    c_h = jnp.concatenate([v[i, 2 * nl : 3 * nl] for v, _, i in parts], 0)
    w_d = jnp.concatenate([w[i, 2 * nl :] for _, w, i in parts], 0)
    c_gu = jnp.concatenate([v[i, : 2 * nl] for v, _, i in parts], 0)
    w_gu = jnp.concatenate([w[i, : 2 * nl] for _, w, i in parts], 0)
    q = sum(v[i, 3 * nl :].astype(F32) for v, _, i in parts)
    q = jnp.concatenate([q, jnp.zeros_like(q)], 0).T.astype(BF)
    tok = own.shape[1]
    out = mm(c_h, w_d, ((0,), (0,))).astype(BF)
    dx = mm(c_gu, w_gu, ((0,), (0,))).astype(BF)
    for k, ref in enumerate((own, *outs)):
        for j in range(NZ):
            rows = slice((k * NZ + j) * tok, (k * NZ + j + 1) * tok)
            ref[order[j], :, :lw] = out[rows]
            ref[order[j], :, lw : 2 * lw] = dx[rows]
            ref[order[j], :, 2 * lw :] = q[rows]


def combine(order, near, far, w_near, w_far):
    n_tok = near.shape[2]
    lw = w_near.shape[2]
    tok = n_tok // (NX * NZ)
    shape = jax.ShapeDtypeStruct((NZ, tok, 2 * lw + 2 * EXPERTS), BF)
    return pl.pallas_call(
        combine_kernel,
        out_shape=(shape,) * NX,
        in_specs=[pl.BlockSpec(memory_space=pltpu.SMEM)]
        + [pl.BlockSpec(memory_space=pltpu.VMEM)] * 4,
        cost_estimate=pl.CostEstimate(
            flops=2 * n_tok * 8 * w_near.shape[1] * lw,
            bytes_accessed=8 * 1024 * 1024,
            transcendentals=0,
        ),
        compiler_params=pltpu.CompilerParams(vmem_limit_bytes=40 * 1024 * 1024),
    )(order, near, far, w_near, w_far)


def reduce_ep(parts):
    moved = [move_x(parts[s], s) for s in range(1, NX)]
    total = parts[0].astype(F32)
    for m in moved:
        total = total + m.astype(F32)
    total = total.astype(BF)
    groups = [[z * NX + x for z in range(NZ)] for x in range(NX)]
    got = lax.all_to_all(
        total, "ep", split_axis=0, concat_axis=0, tiled=True,
        axis_index_groups=groups,
    )
    return jnp.sum(got.astype(F32), 0)


def gather_rows(v):
    near = [v] + [move_y(v, -s) for s in range(1, NY)]
    return near, [swap_core(n) for n in near]


def grads_kernel(cols, got, select, *refs):
    rows = refs[:8]
    outs = refs[8:11]
    buf, sem = refs[11:]
    lw = rows[0].shape[1] // 2
    n_tok = select.shape[0]
    n_out = E_DEV * CAPN
    slot = got[:, 3 * n_tok : 3 * n_tok + n_out].astype(jnp.int32) - 1
    placing = jnp.where(slot == lax.broadcasted_iota(jnp.int32, slot.shape, 1), 1.0, 0.0).astype(BF)
    compact = []
    for i in range(3):
        placed = mm(placing, got[:, i * n_tok : (i + 1) * n_tok], ((0,), (0,))).astype(BF)
        compact.append(
            [
                mm(
                    placed[e * CAPN : (e + 1) * CAPN],
                    select[:, e * TCAP : (e + 1) * TCAP],
                    ((1,), (0,)),
                ).astype(BF)
                for e in range(E_DEV)
            ]
        )
    copies = []
    for j in range(8):
        col = pl.multiple_of(cols[j] * lw, lw)
        for e in range(E_DEV):
            span = slice(e * TCAP, (e + 1) * TCAP)
            both = jnp.concatenate([compact[0][e], compact[1][e]], 0)
            res = mm(both, rows[j][span, :lw], ((1,), (0,))).astype(BF)
            buf[j, 0, e] = res[:CAPN]
            buf[j, 1, e] = res[CAPN:]
            buf[j, 2, e] = mm(compact[2][e], rows[j][span, lw:], ((1,), (0,))).astype(BF)
        for i in range(3):
            copy = pltpu.make_async_copy(
                buf.at[j, i], outs[i].at[:, :, pl.ds(col, lw)], sem.at[j, i]
            )
            copy.start()
            copies.append(copy)
    for copy in copies:
        copy.wait()


def expert_grads(cols, got, select, rows):
    lw = rows[0].shape[1] // 2
    shape = jax.ShapeDtypeStruct((E_DEV, CAPN, 8 * lw), BF)
    vmem = pl.BlockSpec(memory_space=pltpu.VMEM)
    return pl.pallas_call(
        grads_kernel,
        out_shape=(shape, shape, shape),
        in_specs=[pl.BlockSpec(memory_space=pltpu.SMEM)] + [vmem] * 10,
        out_specs=(pl.BlockSpec(memory_space=pl.ANY),) * 3,
        scratch_shapes=[
            pltpu.VMEM((8, 3, E_DEV, CAPN, lw), BF),
            pltpu.SemaphoreType.DMA((8, 3)),
        ],
        cost_estimate=pl.CostEstimate(
            flops=6 * E_DEV * CAPN * TCAP * 8 * lw,
            bytes_accessed=16 * 1024 * 1024,
            transcendentals=0,
        ),
        compiler_params=pltpu.CompilerParams(vmem_limit_bytes=40 * 1024 * 1024),
    )(cols, got, select, *rows)


def body(
    tokens,
    cotangent,
    w_gate,
    w_up,
    w_down,
    neuron_expert,
    neuron_slot,
    choice_expert,
    choice_weight,
):
    t = lax.axis_index("tp")
    ep = lax.axis_index("ep")
    y, c = t // 2, t % 2
    z, x = ep // NX, ep % NX
    n_ep = NX * NZ
    nl, width = w_gate.shape
    tok = tokens.shape[0]
    lw = width // (2 * NY)
    n_tok = n_ep * tok

    experts = lax.broadcasted_iota(jnp.int32, (tok, choice_expert.shape[1], EXPERTS), 2)
    picked = choice_expert[:, :, None] == experts
    dense_w = jnp.sum(jnp.where(picked, choice_weight[:, :, None], 0.0), 1)
    w_hi = dense_w.astype(BF)
    w_lo = (dense_w - w_hi.astype(F32)).astype(BF)
    block = jnp.concatenate(
        [
            lax.dynamic_slice_in_dim(tokens, t * lw, lw, 1),
            lax.dynamic_slice_in_dim(cotangent, t * lw, lw, 1),
            w_hi,
            w_lo,
        ],
        1,
    )
    rows = gather_tokens(block).reshape(n_tok, 2 * lw + 2 * EXPERTS)
    xs = rows[:, :lw]
    cs = rows[:, lw : 2 * lw]
    hi = rows[:, 2 * lw : 2 * lw + EXPERTS]
    lo = rows[:, 2 * lw + EXPERTS :]
    w_near, w_far = exchange_weights(w_gate, w_up, w_down, y, c)

    def partial_sums(w):
        gu = mm(w[:, : 2 * nl].reshape(-1, lw), xs, ((1,), (1,))).reshape(NY, 2 * nl, n_tok)
        d = mm(w[:, 2 * nl :].reshape(-1, lw), cs, ((1,), (1,))).reshape(NY, nl, n_tok)
        return jnp.concatenate([gu, d], 1)

    far_sums = partial_sums(w_far)
    sums = reduce_tp(partial_sums(w_near), far_sums)
    gate, upper, d_raw = sums[:nl], sums[nl : 2 * nl], sums[2 * nl :]

    onehot = (
        neuron_expert[:, None] == lax.broadcasted_iota(jnp.int32, (nl, EXPERTS), 1)
    ).astype(BF)
    scale = mm(onehot, hi, ((1,), (1,))) + mm(onehot, lo, ((1,), (1,)))
    sig = jax.nn.sigmoid(gate)
    silu = gate * sig
    hidden = silu * upper
    dh = d_raw * scale
    coefs = jnp.concatenate(
        [dh * upper * sig * (1.0 + gate * (1.0 - sig)), dh * silu, hidden * scale], 0
    ).astype(BF)
    q_exp = mm(onehot, (hidden * d_raw).astype(BF), ((0,), (0,))).astype(BF)

    near_coefs, far_coefs = gather_tp(jnp.concatenate([coefs, q_exp], 0))
    order = (z + jnp.arange(NZ, dtype=jnp.int32)) % NZ
    parts = combine(order, near_coefs, far_coefs, w_near, w_far)
    final = reduce_ep(parts)
    output = final[:, :lw].astype(BF)
    d_tokens = final[:, lw : 2 * lw].astype(BF)
    q_mine = final[:, 2 * lw : 2 * lw + EXPERTS]
    d_weight = jnp.sum(jnp.where(picked, q_mine[:, None, :], 0.0), 2)

    ri = lax.broadcasted_iota(jnp.int32, (n_tok, n_tok), 0)
    ci = lax.broadcasted_iota(jnp.int32, (n_tok, n_tok), 1)
    per_x = n_tok // NX
    place = (ri // per_x + x) % NX * per_x + (ri // tok % NZ + z) % NZ * tok + ri % tok
    to_common = (place == ci).astype(BF)
    earlier = (ci <= ri).astype(BF)
    own = lax.broadcasted_iota(jnp.int32, (EXPERTS, E_DEV), 0) == (
        ep * E_DEV + lax.broadcasted_iota(jnp.int32, (EXPERTS, E_DEV), 1)
    )
    chosen = (mm(hi, own.astype(BF), ((1,), (0,))) > 0.0).astype(BF)
    rank = mm(earlier, chosen, ((1,), (0,))).astype(jnp.int32) - 1
    slots = lax.broadcasted_iota(jnp.int32, (n_tok, TCAP), 1)
    select = jnp.concatenate(
        [
            jnp.where((rank[:, i : i + 1] == slots) & (chosen[:, i : i + 1] > 0), 1.0, 0.0)
            for i in range(E_DEV)
        ],
        1,
    ).astype(BF)
    select_common = mm(to_common, select, ((0,), (0,))).astype(BF)
    after_coefs = near_coefs[1, 0, 0].astype(F32) * 0.0
    chosen_rows = (mm(select, rows[:, : 2 * lw], ((0,), (0,))) + after_coefs).astype(BF)
    near_rows, far_rows = gather_rows(chosen_rows)

    owner = neuron_expert // E_DEV
    row_i = lax.broadcasted_iota(jnp.int32, (nl, nl), 0)
    col_i = lax.broadcasted_iota(jnp.int32, (nl, nl), 1)
    before = jnp.sum(((owner[:, None] == owner[None, :]) & (col_i < row_i)).astype(jnp.int32), 1)
    target = owner * PEER + before
    packing = (
        target[None, :] == lax.broadcasted_iota(jnp.int32, (n_ep * PEER, nl), 0)
    ).astype(BF)
    label = (neuron_expert % E_DEV * CAPN + neuron_slot + 1).astype(BF)
    common = mm(coefs, to_common, ((1,), (0,))).astype(BF)
    packed = [mm(packing, common[i * nl : (i + 1) * nl], ((1,), (0,))).astype(BF) for i in range(3)]
    tag = jnp.broadcast_to(label[:, None], (nl, 128))
    packed.append(mm(packing, tag, ((1,), (0,))).astype(BF))
    sent = jnp.concatenate(packed, 1).reshape(n_ep, PEER, -1)
    got = lax.all_to_all(sent, "ep", split_axis=0, concat_axis=0, tiled=True)
    got = got.reshape(n_ep * PEER, -1)
    turns = jnp.arange(8, dtype=jnp.int32)
    cols = (y + turns % NY) % NY * 2 + (c + turns // NY) % 2
    grads = expert_grads(cols, got, select_common, near_rows + far_rows)
    return output, d_tokens, d_weight, grads[0], grads[1], grads[2]


def solution(mesh):
    in_specs = (
        P("ep", None),
        P("ep", None),
        P(("tp", "ep"), None),
        P(("tp", "ep"), None),
        P(("tp", "ep"), None),
        P(("tp", "ep")),
        P(("tp", "ep")),
        P("ep", None),
        P("ep", None),
    )
    out_specs = (
        P("ep", "tp"),
        P("ep", "tp"),
        P("ep", None),
        P("ep", "tp", None),
        P("ep", "tp", None),
        P("ep", "tp", None),
    )

    return jax.shard_map(body, mesh=mesh, in_specs=in_specs, out_specs=out_specs, check_vma=False)
```

profile of v0, /device:TPU:2, one launch (start us, length us, event | category | flops | bytes accessed | tf_op | source)
XLA Modules:
  0.0 169.0 jit_solution(5283231985018746693)
XLA Ops:
  4.8 2.8 %collective-permute-start.4 = (bf16[16,2176]{1,0:T(8,128)(2,1)S(1)}, bf16[16,2176]{1,0:T(8,128)(2,1)S(1)}, u32[]{:S(2)}, u32[]{:S(2)}) collective-permute-start(bf16[16,2176]{1,0:T(8,128)(2,1)S(1)} %concatenate.44), channel_id=1, source_target_pairs={{0,2},{1,3},{2,0},{3,1},{4,6},{5,7},{6,4},{7,5},{8,10},{9,11},{10,... | collective-permute-start | bytes 208904 | tf_op jit(solution)/shard_map/ppermute | solution.py:23
  9.7 3.3 %collective-permute-start.1 = (bf16[168,2048]{1,0:T(8,128)(2,1)S(1)}, bf16[168,2048]{1,0:T(8,128)(2,1)S(1)}, u32[]{:S(2)}, u32[]{:S(2)}) collective-permute-start(bf16[168,2048]{1,0:T(8,128)(2,1)S(1)} %pad_maximum_fusion.5), channel_id=1, source_target_pairs={{0,128},{32,160},{64,192},{96,224},{128,0},{160,32},{192,64},{224,... | collective-permute-start | bytes 2064392 | tf_op jit(solution)/shard_map/ppermute | solution.py:33
  15.1 2.6 %collective-permute-start = (bf16[168,2048]{1,0:T(8,128)(2,1)S(1)}, bf16[168,2048]{1,0:T(8,128)(2,1)S(1)}, u32[]{:S(2)}, u32[]{:S(2)}) collective-permute-start(bf16[168,2048]{1,0:T(8,128)(2,1)S(1)} %pad_maximum_fusion.4), channel_id=1, source_target_pairs={{0,192},{32,224},{64,0},{96,32},{128,64},{160,96},{192,128},{224,1... | collective-permute-start | bytes 2064392 | tf_op jit(solution)/shard_map/ppermute | solution.py:33
  17.8 5.9 %collective-permute-start.6 = (bf16[4,16,2176]{2,1,0:T(8,128)(2,1)S(1)}, bf16[4,16,2176]{2,1,0:T(8,128)(2,1)S(1)}, u32[]{:S(2)}, u32[]{:S(2)}) collective-permute-start(bf16[4,16,2176]{2,1,0:T(8,128)(2,1)S(1)} %pad_maximum_fusion.9), channel_id=1, source_target_pairs={{0,28},{1,29},{2,30},{3,31},{4,0},{5,1},{6,2},{7,3},{8,4},{9,5},{1... | collective-permute-start | bytes 835592 | tf_op jit(solution)/shard_map/ppermute | solution.py:28
  23.8 4.2 %collective-permute-done.6 = bf16[4,16,2176]{2,1,0:T(8,128)(2,1)S(1)} collective-permute-done((bf16[4,16,2176]{2,1,0:T(8,128)(2,1)S(1)}, bf16[4,16,2176]{2,1,0:T(8,128)(2,1)S(1)}, u32[]{:S(2)}, u32[]{:S(2)}) %collective-permute-start.6) | collective-permute-done | bytes 278560 | tf_op jit(solution)/shard_map/ppermute | solution.py:28
  28.0 3.7 %collective-permute-start.7 = (bf16[4,16,2176]{2,1,0:T(8,128)(2,1)S(1)}, bf16[4,16,2176]{2,1,0:T(8,128)(2,1)S(1)}, u32[]{:S(2)}, u32[]{:S(2)}) collective-permute-start(bf16[4,16,2176]{2,1,0:T(8,128)(2,1)S(1)} %collective-permute-done.6), channel_id=1, source_target_pairs={{0,28},{1,29},{2,30},{3,31},{4,0},{5,1},{6,2},{7,3},{8,4},{9,5},{1... | collective-permute-start | bytes 835592 | tf_op jit(solution)/shard_map/ppermute | solution.py:28
  31.7 4.0 %collective-permute-done.7 = bf16[4,16,2176]{2,1,0:T(8,128)(2,1)S(1)} collective-permute-done((bf16[4,16,2176]{2,1,0:T(8,128)(2,1)S(1)}, bf16[4,16,2176]{2,1,0:T(8,128)(2,1)S(1)}, u32[]{:S(2)}, u32[]{:S(2)}) %collective-permute-start.7) | collective-permute-done | bytes 278560 | tf_op jit(solution)/shard_map/ppermute | solution.py:28
  35.8 3.7 %collective-permute-start.8 = (bf16[4,16,2176]{2,1,0:T(8,128)(2,1)S(1)}, bf16[4,16,2176]{2,1,0:T(8,128)(2,1)S(1)}, u32[]{:S(2)}, u32[]{:S(2)}) collective-permute-start(bf16[4,16,2176]{2,1,0:T(8,128)(2,1)S(1)} %collective-permute-done.7), channel_id=1, source_target_pairs={{0,28},{1,29},{2,30},{3,31},{4,0},{5,1},{6,2},{7,3},{8,4},{9,5},{1... | collective-permute-start | bytes 835592 | tf_op jit(solution)/shard_map/ppermute | solution.py:28
  39.6 2.9 %collective-permute-done.2 = bf16[168,2048]{1,0:T(8,128)(2,1)} collective-permute-done((bf16[168,2048]{1,0:T(8,128)(2,1)}, bf16[168,2048]{1,0:T(8,128)(2,1)}, u32[]{:S(2)}, u32[]{:S(2)}) %collective-permute-start.2) | collective-permute-done | bytes 688160 | tf_op jit(solution)/shard_map/ppermute | solution.py:33
  44.2 5.9 %collective-permute-start.9 = (bf16[2,16,2176]{2,1,0:T(8,128)(2,1)S(1)}, bf16[2,16,2176]{2,1,0:T(8,128)(2,1)S(1)}, u32[]{:S(2)}, u32[]{:S(2)}) collective-permute-start(bf16[2,16,2176]{2,1,0:T(8,128)(2,1)S(1)} %slice.122), channel_id=1, source_target_pairs={{0,28},{1,29},{2,30},{3,31},{4,0},{5,1},{6,2},{7,3},{8,4},{9,5},{1... | collective-permute-start | bytes 417800 | tf_op jit(solution)/shard_map/ppermute | solution.py:28
  50.4 3.3 %collective-permute-done.9 = bf16[2,16,2176]{2,1,0:T(8,128)(2,1)S(1)} collective-permute-done((bf16[2,16,2176]{2,1,0:T(8,128)(2,1)S(1)}, bf16[2,16,2176]{2,1,0:T(8,128)(2,1)S(1)}, u32[]{:S(2)}, u32[]{:S(2)}) %collective-permute-start.9) | collective-permute-done | bytes 139296 | tf_op jit(solution)/shard_map/ppermute | solution.py:28
  53.7 3.7 %collective-permute-done.13 = bf16[2,16,2176]{2,1,0:T(8,128)(2,1)S(1)} collective-permute-done((bf16[2,16,2176]{2,1,0:T(8,128)(2,1)S(1)}, bf16[2,16,2176]{2,1,0:T(8,128)(2,1)S(1)}, u32[]{:S(2)}, u32[]{:S(2)}) %collective-permute-start.13) | collective-permute-done | bytes 139296 | tf_op jit(solution)/shard_map/ppermute | solution.py:28
  67.2 2.7 %collective-permute-done.16 = bf16[168,512]{1,0:T(8,128)(2,1)S(1)} collective-permute-done((bf16[168,512]{1,0:T(8,128)(2,1)S(1)}, bf16[168,512]{1,0:T(8,128)(2,1)S(1)}, u32[]{:S(2)}, u32[]{:S(2)}) %collective-permute-start.16) | collective-permute-done | bytes 172064 | tf_op jit(solution)/shard_map/ppermute | solution.py:33
  71.0 2.6 %collective-permute-done.17 = bf16[168,512]{1,0:T(8,128)(2,1)S(1)} collective-permute-done((bf16[168,512]{1,0:T(8,128)(2,1)S(1)}, bf16[168,512]{1,0:T(8,128)(2,1)S(1)}, u32[]{:S(2)}, u32[]{:S(2)}) %collective-permute-start.17) | collective-permute-done | bytes 172064 | tf_op jit(solution)/shard_map/ppermute | solution.py:33
  78.8 8.8 %collective-permute-done.19 = bf16[232,512]{1,0:T(8,128)(2,1)S(1)} collective-permute-done((bf16[232,512]{1,0:T(8,128)(2,1)S(1)}, bf16[232,512]{1,0:T(8,128)(2,1)S(1)}, u32[]{:S(2)}, u32[]{:S(2)}) %collective-permute-start.19) | collective-permute-done | bytes 237600 | tf_op jit(solution)/shard_map/ppermute | solution.py:33
  92.5 2.7 %collective-permute-start.27 = (bf16[256,2048]{1,0:T(8,128)(2,1)S(1)}, bf16[256,2048]{1,0:T(8,128)(2,1)}, u32[]{:S(2)}, u32[]{:S(2)}) collective-permute-start(bf16[256,2048]{1,0:T(8,128)(2,1)S(1)} %fusion.refs_0_), channel_id=1, source_target_pairs={{0,128},{32,160},{64,192},{96,224},{128,0},{160,32},{192,64},{224,... | collective-permute-start | bytes 3145736 | tf_op jit(solution)/shard_map/ppermute | solution.py:33
  96.0 3.5 %shard_map.136 = (bf16[8,16,2176]{2,1,0:T(8,128)(2,1)S(1)}, bf16[8,16,2176]{2,1,0:T(8,128)(2,1)}, bf16[8,16,2176]{2,1,0:T(8,128)(2,1)}, bf16[8,16,2176]{2,1,0:T(8,128)(2,1)}) custom-call(s32[8]{0:T(128)S(1)} %and_select_fusion.6.order, bf16[4,232,512]{2,1,0:T(8,128)(2,1)S(1)} %pad_maximum_fusion.2.near, ...), custom_call_target="tpu_custom_call" | custom-call | flops 1409286144 | bytes 8388608 | tf_op jit(solution)/shard_map/pallas_call | solution.py:115
  99.5 3.5 %collective-permute-start.24 = (bf16[8,16,2176]{2,1,0:T(8,128)(2,1)}, bf16[8,16,2176]{2,1,0:T(8,128)(2,1)}, u32[]{:S(2)}, u32[]{:S(2)}) collective-permute-start(bf16[8,16,2176]{2,1,0:T(8,128)(2,1)} %get-tuple-element.15), channel_id=1, source_target_pairs={{0,2},{1,3},{2,0},{3,1},{4,6},{5,7},{6,4},{7,5},{8,10},{9,11},{10,... | collective-permute-start | bytes 1671176 | tf_op jit(solution)/shard_map/ppermute | solution.py:23
  103.0 13.6 %collective-permute-done.28.refs_3_ = bf16[256,2048]{1,0:T(8,128)(2,1)S(1)} collective-permute-done((bf16[256,2048]{1,0:T(8,128)(2,1)S(1)}, bf16[256,2048]{1,0:T(8,128)(2,1)S(1)}, u32[]{:S(2)}, u32[]{:S(2)}) %collective-permute-start.28) | collective-permute-done | bytes 1048608 | tf_op jit(solution)/shard_map/ppermute | solution.py:33
  119.3 5.2 %all-to-all-start.1 = ((bf16[32,4,1664]{2,1,0:T(4,128)(2,1)}), bf16[32,4,1664]{2,1,0:T(4,128)(2,1)S(1)}, u32[]{:S(2)}, u32[]{:S(2)}) async-start(bf16[32,4,1664]{2,1,0:T(4,128)(2,1)} %reshape.52), calls=%async_computation.1 | async-start | bytes 851968 | tf_op jit(solution)/shard_map/all_to_all | solution.py:323
  124.5 15.5 %collective-permute-done.27.refs_2_ = bf16[256,2048]{1,0:T(8,128)(2,1)} collective-permute-done((bf16[256,2048]{1,0:T(8,128)(2,1)S(1)}, bf16[256,2048]{1,0:T(8,128)(2,1)}, u32[]{:S(2)}, u32[]{:S(2)}) %collective-permute-start.27) | collective-permute-done | bytes 1048608 | tf_op jit(solution)/shard_map/ppermute | solution.py:33
  144.8 3.5 %all-to-all-start = ((bf16[8,16,2176]{2,1,0:T(8,128)(2,1)}), bf16[8,16,2176]{2,1,0:T(8,128)(2,1)S(1)}, u32[]{:S(2)}, u32[]{:S(2)}) async-start(bf16[8,16,2176]{2,1,0:T(8,128)(2,1)} %add_convert_fusion), calls=%async_computation | async-start | bytes 1114112 | tf_op jit(solution)/shard_map/all_to_all | solution.py:136
  150.6 6.6 %shard_map.137 = (bf16[2,64,8192]{2,1,0:T(8,128)(2,1)}, bf16[2,64,8192]{2,1,0:T(8,128)(2,1)}, bf16[2,64,8192]{2,1,0:T(8,128)(2,1)}) custom-call(s32[8]{0:T(128)S(1)} %fusion.55.cols, bf16[128,1664]{1,0:T(8,128)(2,1)S(1)} %reshape.53.got, bf16[512,256]{1,0:T(8,128)(2,1)S(1)} %convolution_convert_fusion.1.select, bf16[256,2048]{1,0:T(8,128)(2,1)S(1)} %fusion.refs_0_, ...), custom_call_target="tpu_custom_call" | custom-call | flops 805306368 | bytes 16777216 | tf_op jit(solution)/shard_map/pallas_call | solution.py:194
  157.2 10.2 %all-to-all-done = bf16[8,16,2176]{2,1,0:T(8,128)(2,1)S(1)} async-done(((bf16[8,16,2176]{2,1,0:T(8,128)(2,1)}), bf16[8,16,2176]{2,1,0:T(8,128)(2,1)S(1)}, u32[]{:S(2)}, u32[]{:S(2)}) %all-to-all-start) | async-done | bytes 557088 | tf_op jit(solution)/shard_map/all_to_all | solution.py:136
  (136 shorter events, 42.5 us)
Async XLA Ops:
  3.3 11.8 %collective-permute-start.5 = (bf16[16,2176]{1,0:T(8,128)(2,1)S(1)}, bf16[16,2176]{1,0:T(8,128)(2,1)S(1)}, u32[]{:S(2)}, u32[]{:S(2)}) collective-permute-start(bf16[16,2176]{1,0:T(8,128)(2,1)S(1)} %concatenate.44), channel_id=1, source_target_pairs={{0,1},{1,2},{2,3},{3,0},{4,5},{5,6},{6,7},{7,4},{8,9},{9,10},{10,1... | collective-permute-start | bytes 208904 | tf_op jit(solution)/shard_map/ppermute | solution.py:23
  4.8 13.0 %collective-permute-start.4 = (bf16[16,2176]{1,0:T(8,128)(2,1)S(1)}, bf16[16,2176]{1,0:T(8,128)(2,1)S(1)}, u32[]{:S(2)}, u32[]{:S(2)}) collective-permute-start(bf16[16,2176]{1,0:T(8,128)(2,1)S(1)} %concatenate.44), channel_id=1, source_target_pairs={{0,2},{1,3},{2,0},{3,1},{4,6},{5,7},{6,4},{7,5},{8,10},{9,11},{10,... | collective-permute-start | bytes 208904 | tf_op jit(solution)/shard_map/ppermute | solution.py:23
  7.6 10.2 %collective-permute-start.3 = (bf16[16,2176]{1,0:T(8,128)(2,1)S(1)}, bf16[16,2176]{1,0:T(8,128)(2,1)S(1)}, u32[]{:S(2)}, u32[]{:S(2)}) collective-permute-start(bf16[16,2176]{1,0:T(8,128)(2,1)S(1)} %concatenate.44), channel_id=1, source_target_pairs={{0,3},{1,0},{2,1},{3,2},{4,7},{5,4},{6,5},{7,6},{8,11},{9,8},{10,9... | collective-permute-start | bytes 208904 | tf_op jit(solution)/shard_map/ppermute | solution.py:23
  9.7 29.8 %collective-permute-start.1 = (bf16[168,2048]{1,0:T(8,128)(2,1)S(1)}, bf16[168,2048]{1,0:T(8,128)(2,1)S(1)}, u32[]{:S(2)}, u32[]{:S(2)}) collective-permute-start(bf16[168,2048]{1,0:T(8,128)(2,1)S(1)} %pad_maximum_fusion.5), channel_id=1, source_target_pairs={{0,128},{32,160},{64,192},{96,224},{128,0},{160,32},{192,64},{224,... | collective-permute-start | bytes 2064392 | tf_op jit(solution)/shard_map/ppermute | solution.py:33
  13.9 28.6 %collective-permute-start.2 = (bf16[168,2048]{1,0:T(8,128)(2,1)}, bf16[168,2048]{1,0:T(8,128)(2,1)}, u32[]{:S(2)}, u32[]{:S(2)}) collective-permute-start(bf16[168,2048]{1,0:T(8,128)(2,1)} %pad_maximum_fusion.6), channel_id=1, source_target_pairs={{0,64},{32,96},{64,128},{96,160},{128,192},{160,224},{192,0},{224,... | collective-permute-start | bytes 2064392 | tf_op jit(solution)/shard_map/ppermute | solution.py:33
  15.1 28.5 %collective-permute-start = (bf16[168,2048]{1,0:T(8,128)(2,1)S(1)}, bf16[168,2048]{1,0:T(8,128)(2,1)S(1)}, u32[]{:S(2)}, u32[]{:S(2)}) collective-permute-start(bf16[168,2048]{1,0:T(8,128)(2,1)S(1)} %pad_maximum_fusion.4), channel_id=1, source_target_pairs={{0,192},{32,224},{64,0},{96,32},{128,64},{160,96},{192,128},{224,1... | collective-permute-start | bytes 2064392 | tf_op jit(solution)/shard_map/ppermute | solution.py:33
  17.8 10.2 %collective-permute-start.6 = (bf16[4,16,2176]{2,1,0:T(8,128)(2,1)S(1)}, bf16[4,16,2176]{2,1,0:T(8,128)(2,1)S(1)}, u32[]{:S(2)}, u32[]{:S(2)}) collective-permute-start(bf16[4,16,2176]{2,1,0:T(8,128)(2,1)S(1)} %pad_maximum_fusion.9), channel_id=1, source_target_pairs={{0,28},{1,29},{2,30},{3,31},{4,0},{5,1},{6,2},{7,3},{8,4},{9,5},{1... | collective-permute-start | bytes 835592 | tf_op jit(solution)/shard_map/ppermute | solution.py:28
  39.5 10.7 %collective-permute-start.12 = (bf16[4,16,2176]{2,1,0:T(8,128)(2,1)S(1)}, bf16[4,16,2176]{2,1,0:T(8,128)(2,1)S(1)}, u32[]{:S(2)}, u32[]{:S(2)}) collective-permute-start(bf16[4,16,2176]{2,1,0:T(8,128)(2,1)S(1)} %collective-permute-done.11), channel_id=1, source_target_pairs={{0,4},{1,5},{2,6},{3,7},{4,8},{5,9},{6,10},{7,11},{8,12},{9,13},{1... | collective-permute-start | bytes 835592 | tf_op jit(solution)/shard_map/ppermute | solution.py:28
  43.9 14.2 %collective-permute-start.14 = (bf16[4,168,1024]{2,1,0:T(8,128)(2,1)S(1)}, bf16[4,168,1024]{2,1,0:T(8,128)(2,1)S(1)}, u32[]{:S(2)}, u32[]{:S(2)}) collective-permute-start(bf16[4,168,1024]{2,1,0:T(8,128)(2,1)S(1)} %pad_maximum_fusion.1), channel_id=1, source_target_pairs={{0,32},{32,0},{64,96},{96,64},{128,160},{160,128},{192,224},{224,1... | collective-permute-start | bytes 4128776 | tf_op jit(solution)/shard_map/ppermute | solution.py:37
  44.2 9.5 %collective-permute-start.9 = (bf16[2,16,2176]{2,1,0:T(8,128)(2,1)S(1)}, bf16[2,16,2176]{2,1,0:T(8,128)(2,1)S(1)}, u32[]{:S(2)}, u32[]{:S(2)}) collective-permute-start(bf16[2,16,2176]{2,1,0:T(8,128)(2,1)S(1)} %slice.122), channel_id=1, source_target_pairs={{0,28},{1,29},{2,30},{3,31},{4,0},{5,1},{6,2},{7,3},{8,4},{9,5},{1... | collective-permute-start | bytes 417800 | tf_op jit(solution)/shard_map/ppermute | solution.py:28
  74.2 13.9 %collective-permute-start.20 = (bf16[232,512]{1,0:T(8,128)(2,1)S(1)}, bf16[232,512]{1,0:T(8,128)(2,1)S(1)}, u32[]{:S(2)}, u32[]{:S(2)}) collective-permute-start(bf16[232,512]{1,0:T(8,128)(2,1)S(1)} %get-tuple-element.59), channel_id=1, source_target_pairs={{0,128},{32,160},{64,192},{96,224},{128,0},{160,32},{192,64},{224,... | collective-permute-start | bytes 712712 | tf_op jit(solution)/shard_map/ppermute | solution.py:33
  76.1 11.5 %collective-permute-start.19 = (bf16[232,512]{1,0:T(8,128)(2,1)S(1)}, bf16[232,512]{1,0:T(8,128)(2,1)S(1)}, u32[]{:S(2)}, u32[]{:S(2)}) collective-permute-start(bf16[232,512]{1,0:T(8,128)(2,1)S(1)} %get-tuple-element.59), channel_id=1, source_target_pairs={{0,192},{32,224},{64,0},{96,32},{128,64},{160,96},{192,128},{224,1... | collective-permute-start | bytes 712712 | tf_op jit(solution)/shard_map/ppermute | solution.py:33
  78.4 9.7 %collective-permute-start.21 = (bf16[232,512]{1,0:T(8,128)(2,1)S(1)}, bf16[232,512]{1,0:T(8,128)(2,1)S(1)}, u32[]{:S(2)}, u32[]{:S(2)}) collective-permute-start(bf16[232,512]{1,0:T(8,128)(2,1)S(1)} %get-tuple-element.59), channel_id=1, source_target_pairs={{0,64},{32,96},{64,128},{96,160},{128,192},{160,224},{192,0},{224,... | collective-permute-start | bytes 712712 | tf_op jit(solution)/shard_map/ppermute | solution.py:33
  89.8 26.9 %collective-permute-start.28 = (bf16[256,2048]{1,0:T(8,128)(2,1)S(1)}, bf16[256,2048]{1,0:T(8,128)(2,1)S(1)}, u32[]{:S(2)}, u32[]{:S(2)}) collective-permute-start(bf16[256,2048]{1,0:T(8,128)(2,1)S(1)} %fusion.refs_0_), channel_id=1, source_target_pairs={{0,64},{32,96},{64,128},{96,160},{128,192},{160,224},{192,0},{224,... | collective-permute-start | bytes 3145736 | tf_op jit(solution)/shard_map/ppermute | solution.py:33
  92.5 47.6 %collective-permute-start.27 = (bf16[256,2048]{1,0:T(8,128)(2,1)S(1)}, bf16[256,2048]{1,0:T(8,128)(2,1)}, u32[]{:S(2)}, u32[]{:S(2)}) collective-permute-start(bf16[256,2048]{1,0:T(8,128)(2,1)S(1)} %fusion.refs_0_), channel_id=1, source_target_pairs={{0,128},{32,160},{64,192},{96,224},{128,0},{160,32},{192,64},{224,... | collective-permute-start | bytes 3145736 | tf_op jit(solution)/shard_map/ppermute | solution.py:33
  95.1 45.9 %collective-permute-start.26 = (bf16[256,2048]{1,0:T(8,128)(2,1)S(1)}, bf16[256,2048]{1,0:T(8,128)(2,1)}, u32[]{:S(2)}, u32[]{:S(2)}) collective-permute-start(bf16[256,2048]{1,0:T(8,128)(2,1)S(1)} %fusion.refs_0_), channel_id=1, source_target_pairs={{0,192},{32,224},{64,0},{96,32},{128,64},{160,96},{192,128},{224,1... | collective-permute-start | bytes 3145736 | tf_op jit(solution)/shard_map/ppermute | solution.py:33
  99.5 41.5 %collective-permute-start.23 = (bf16[8,16,2176]{2,1,0:T(8,128)(2,1)}, bf16[8,16,2176]{2,1,0:T(8,128)(2,1)}, u32[]{:S(2)}, u32[]{:S(2)}) collective-permute-start(bf16[8,16,2176]{2,1,0:T(8,128)(2,1)} %get-tuple-element.14), channel_id=1, source_target_pairs={{0,1},{1,2},{2,3},{3,0},{4,5},{5,6},{6,7},{7,4},{8,9},{9,10},{10,1... | collective-permute-start | bytes 1671176 | tf_op jit(solution)/shard_map/ppermute | solution.py:23
  99.5 42.0 %collective-permute-start.24 = (bf16[8,16,2176]{2,1,0:T(8,128)(2,1)}, bf16[8,16,2176]{2,1,0:T(8,128)(2,1)}, u32[]{:S(2)}, u32[]{:S(2)}) collective-permute-start(bf16[8,16,2176]{2,1,0:T(8,128)(2,1)} %get-tuple-element.15), channel_id=1, source_target_pairs={{0,2},{1,3},{2,0},{3,1},{4,6},{5,7},{6,4},{7,5},{8,10},{9,11},{10,... | collective-permute-start | bytes 1671176 | tf_op jit(solution)/shard_map/ppermute | solution.py:23
  116.6 25.0 %collective-permute-start.25 = (bf16[8,16,2176]{2,1,0:T(8,128)(2,1)}, bf16[8,16,2176]{2,1,0:T(8,128)(2,1)}, u32[]{:S(2)}, u32[]{:S(2)}) collective-permute-start(bf16[8,16,2176]{2,1,0:T(8,128)(2,1)} %get-tuple-element.16), channel_id=1, source_target_pairs={{0,3},{1,0},{2,1},{3,2},{4,7},{5,4},{6,5},{7,6},{8,11},{9,8},{10,9... | collective-permute-start | bytes 1671176 | tf_op jit(solution)/shard_map/ppermute | solution.py:23
  119.3 24.7 %all-to-all-start.1 = ((bf16[32,4,1664]{2,1,0:T(4,128)(2,1)}), bf16[32,4,1664]{2,1,0:T(4,128)(2,1)S(1)}, u32[]{:S(2)}, u32[]{:S(2)}) async-start(bf16[32,4,1664]{2,1,0:T(4,128)(2,1)} %reshape.52), calls=%async_computation.1 | async-start | bytes 851968 | tf_op jit(solution)/shard_map/all_to_all | solution.py:323
  140.1 10.6 %collective-permute-start.29 = (bf16[256,2048]{1,0:T(8,128)(2,1)S(1)}, bf16[256,2048]{1,0:T(8,128)(2,1)}, u32[]{:S(2)}, u32[]{:S(2)}) collective-permute-start(bf16[256,2048]{1,0:T(8,128)(2,1)S(1)} %fusion.refs_0_), channel_id=1, source_target_pairs={{0,32},{32,0},{64,96},{96,64},{128,160},{160,128},{192,224},{224,1... | collective-permute-start | bytes 3145736 | tf_op jit(solution)/shard_map/ppermute | solution.py:37
  141.0 9.6 %collective-permute-start.32 = (bf16[256,2048]{1,0:T(8,128)(2,1)S(1)}, bf16[256,2048]{1,0:T(8,128)(2,1)}, u32[]{:S(2)}, u32[]{:S(2)}) collective-permute-start(bf16[256,2048]{1,0:T(8,128)(2,1)S(1)} %collective-permute-done.28.refs_3_), channel_id=1, source_target_pairs={{0,32},{32,0},{64,96},{96,64},{128,160},{160,128},{192,224},{224,1... | collective-permute-start | bytes 3145736 | tf_op jit(solution)/shard_map/ppermute | solution.py:37
  141.0 9.6 %collective-permute-start.31 = (bf16[256,2048]{1,0:T(8,128)(2,1)}, bf16[256,2048]{1,0:T(8,128)(2,1)}, u32[]{:S(2)}, u32[]{:S(2)}) collective-permute-start(bf16[256,2048]{1,0:T(8,128)(2,1)} %collective-permute-done.27.refs_2_), channel_id=1, source_target_pairs={{0,32},{32,0},{64,96},{96,64},{128,160},{160,128},{192,224},{224,1... | collective-permute-start | bytes 3145736 | tf_op jit(solution)/shard_map/ppermute | solution.py:37
  144.8 22.6 %all-to-all-start = ((bf16[8,16,2176]{2,1,0:T(8,128)(2,1)}), bf16[8,16,2176]{2,1,0:T(8,128)(2,1)S(1)}, u32[]{:S(2)}, u32[]{:S(2)}) async-start(bf16[8,16,2176]{2,1,0:T(8,128)(2,1)} %add_convert_fusion), calls=%async_computation | async-start | bytes 1114112 | tf_op jit(solution)/shard_map/all_to_all | solution.py:136
  (16 other events, 110.2 us)
where the time goes:
time: 171 us; the launch traced here: 169 us
  waiting for transfers between devices  74.3 us (43%)
  starting transfers between devices  59.8 us (35%)
  local copies, waits for them, and re-layouts  10.3 us (6%)
  Pallas kernels  10.1 us (6%)
  matrix products  6.86 us (4%)
  other arithmetic  5.68 us (3%)
  between operations  1.91 us (1%)
    ppermute x12, waiting for transfers between devices, move_y(): return lax.ppermute(v, 'tp', pairs)  48.2 us
    ppermute x12, starting transfers between devices, move_y(): return lax.ppermute(v, 'tp', pairs)  21 us
    ppermute x8, starting transfers between devices, move_z(): return lax.ppermute(v, 'ep', pairs)  19.5 us
    ppermute x8, waiting for transfers between devices, move_z(): return lax.ppermute(v, 'ep', pairs)  15.2 us
    all_to_all x1, waiting for transfers between devices, reduce_ep(): lax.all_to_all(total, 'ep', split_axis=0, concat_axis=0, tiled=True, axis...  10.2 us
    ppermute x6, starting transfers between devices, move_x(): return lax.ppermute(v, 'ep', pairs)  9.7 us
    dot_general x16, matrix products, mm(): return lax.dot_general(a, b, (dims, ((), ())), preferred_element_type=F32)  6.86 us
    pallas_call x1, Pallas kernels, expert_grads(): pl.pallas_call(grads_kernel, out_shape=(shape, shape, shape), in_specs=[p...  6.57 us
  transfers between devices with their start and end apart: 35, of which 14 were waited for; matrix products, arithmetic and copies ran while one was open for 9% of the time, Pallas kernels for 6%

commit v1 on v0

--- a/solution.py
+++ b/solution.py
@@ -86,7 +86,10 @@
     return total
 
 
-def combine_kernel(order, near, far, w_near, w_far, own, *outs):
+def combine_kernel(order, near, far, w_near, w_far, own, *refs):
+    outs = refs[:-1]
+    held = refs[-1]
+    n_blocks = held.shape[0]
     nl = w_near.shape[1] // 3
     lw = w_near.shape[2]
     parts = [(near, w_near, i) for i in range(NY)] + [(far, w_far, i) for i in range(NY)]
@@ -97,14 +100,17 @@
     q = sum(v[i, 3 * nl :].astype(F32) for v, _, i in parts)
     q = jnp.concatenate([q, jnp.zeros_like(q)], 0).T.astype(BF)
     tok = own.shape[1]
-    out = mm(c_h, w_d, ((0,), (0,))).astype(BF)
-    dx = mm(c_gu, w_gu, ((0,), (0,))).astype(BF)
-    for k, ref in enumerate((own, *outs)):
-        for j in range(NZ):
-            rows = slice((k * NZ + j) * tok, (k * NZ + j + 1) * tok)
-            ref[order[j], :, :lw] = out[rows]
-            ref[order[j], :, lw : 2 * lw] = dx[rows]
-            ref[order[j], :, 2 * lw :] = q[rows]
+    whole = (n_blocks, tok)
+    held[:, :, :lw] = mm(c_h, w_d, ((0,), (0,))).astype(BF).reshape(*whole, lw)
+    held[:, :, lw : 2 * lw] = mm(c_gu, w_gu, ((0,), (0,))).astype(BF).reshape(*whole, lw)
+    held[:, :, 2 * lw :] = q.reshape(*whole, 2 * EXPERTS)
+
+    def store(j, carry):
+        for k, ref in enumerate((own, *outs)):
+            ref[order[j]] = held[k * NZ + j]
+        return carry
+
+    lax.fori_loop(0, NZ, store, 0)
 
 
 def combine(order, near, far, w_near, w_far):
@@ -115,6 +121,7 @@
     return pl.pallas_call(
         combine_kernel,
         out_shape=(shape,) * NX,
+        scratch_shapes=[pltpu.VMEM((NX * NZ, *shape.shape[1:]), BF)],
         in_specs=[pl.BlockSpec(memory_space=pltpu.SMEM)]
         + [pl.BlockSpec(memory_space=pltpu.VMEM)] * 4,
         cost_estimate=pl.CostEstimate(
@@ -141,50 +148,64 @@
 
 
 def gather_rows(v):
-    near = [v] + [move_y(v, -s) for s in range(1, NY)]
+    mid = v.shape[0] // 2
+    after = move_y(v, -1)
+    before = move_y(v, 1)
+    via_after = move_y(after[:mid], -1)
+    via_before = move_y(before[mid:], 1)
+    near = [v, after, via_after, via_before, before]
     return near, [swap_core(n) for n in near]
 
 
 def grads_kernel(cols, got, select, *refs):
-    rows = refs[:8]
-    outs = refs[8:11]
-    buf, sem = refs[11:]
-    lw = rows[0].shape[1] // 2
+    rows = refs[:10]
+    outs = refs[10:13]
+    held, coef, buf, in_sem, out_sem = refs[13:]
+    mid = held.shape[1] // 2
+    for h in range(2):
+        part = rows[5 * h : 5 * h + 5]
+        j = NY * h
+        pltpu.make_async_copy(part[0], held.at[j], in_sem.at[j]).start()
+        pltpu.make_async_copy(part[1], held.at[j + 1], in_sem.at[j + 1]).start()
+        pltpu.make_async_copy(part[2], held.at[j + 2, :mid], in_sem.at[j + 2]).start()
+        pltpu.make_async_copy(part[3], held.at[j + 2, mid:], in_sem.at[j + 2]).start()
+        pltpu.make_async_copy(part[4], held.at[j + 3], in_sem.at[j + 3]).start()
+    lw = held.shape[2] // 2
     n_tok = select.shape[0]
     n_out = E_DEV * CAPN
     slot = got[:, 3 * n_tok : 3 * n_tok + n_out].astype(jnp.int32) - 1
     placing = jnp.where(slot == lax.broadcasted_iota(jnp.int32, slot.shape, 1), 1.0, 0.0).astype(BF)
-    compact = []
-    for i in range(3):
-        placed = mm(placing, got[:, i * n_tok : (i + 1) * n_tok], ((0,), (0,))).astype(BF)
-        compact.append(
-            [
-                mm(
-                    placed[e * CAPN : (e + 1) * CAPN],
-                    select[:, e * TCAP : (e + 1) * TCAP],
-                    ((1,), (0,)),
-                ).astype(BF)
-                for e in range(E_DEV)
-            ]
+    placed = mm(placing, got[:, : 3 * n_tok], ((0,), (0,))).astype(BF)
+    for e in range(E_DEV):
+        mine = placed[e * CAPN : (e + 1) * CAPN]
+        stack = jnp.concatenate([mine[:, i * n_tok : (i + 1) * n_tok] for i in range(3)], 0)
+        coef[e] = mm(stack, select[:, e * TCAP : (e + 1) * TCAP], ((1,), (0,))).astype(BF)
+
+    def out_copy(j, i, col):
+        return pltpu.make_async_copy(
+            buf.at[j, i], outs[i].at[:, :, pl.ds(col, lw)], out_sem.at[j, i]
         )
-    copies = []
-    for j in range(8):
+
+    def step(j, carry):
+        pltpu.make_async_copy(rows[0], held.at[j], in_sem.at[j]).wait()
         col = pl.multiple_of(cols[j] * lw, lw)
         for e in range(E_DEV):
             span = slice(e * TCAP, (e + 1) * TCAP)
-            both = jnp.concatenate([compact[0][e], compact[1][e]], 0)
-            res = mm(both, rows[j][span, :lw], ((1,), (0,))).astype(BF)
+            res = mm(coef[e, : 2 * CAPN], held[j, span, :lw], ((1,), (0,))).astype(BF)
             buf[j, 0, e] = res[:CAPN]
             buf[j, 1, e] = res[CAPN:]
-            buf[j, 2, e] = mm(compact[2][e], rows[j][span, lw:], ((1,), (0,))).astype(BF)
+            buf[j, 2, e] = mm(coef[e, 2 * CAPN :], held[j, span, lw:], ((1,), (0,))).astype(BF)
         for i in range(3):
-            copy = pltpu.make_async_copy(
-                buf.at[j, i], outs[i].at[:, :, pl.ds(col, lw)], sem.at[j, i]
-            )
-            copy.start()
-            copies.append(copy)
-    for copy in copies:
-        copy.wait()
+            out_copy(j, i, col).start()
+        return carry
+
+    def drain(j, carry):
+        for i in range(3):
+            out_copy(j, i, 0).wait()
+        return carry
+
+    lax.fori_loop(0, 8, step, 0)
+    lax.fori_loop(0, 8, drain, 0)
 
 
 def expert_grads(cols, got, select, rows):
@@ -194,10 +215,14 @@
     return pl.pallas_call(
         grads_kernel,
         out_shape=(shape, shape, shape),
-        in_specs=[pl.BlockSpec(memory_space=pltpu.SMEM)] + [vmem] * 10,
+        in_specs=[pl.BlockSpec(memory_space=pltpu.SMEM), vmem, vmem]
+        + [pl.BlockSpec(memory_space=pl.ANY)] * 10,
         out_specs=(pl.BlockSpec(memory_space=pl.ANY),) * 3,
         scratch_shapes=[
+            pltpu.VMEM((8, *rows[0].shape), BF),
+            pltpu.VMEM((E_DEV, 3 * CAPN, TCAP), BF),
             pltpu.VMEM((8, 3, E_DEV, CAPN, lw), BF),
+            pltpu.SemaphoreType.DMA((8,)),
             pltpu.SemaphoreType.DMA((8, 3)),
         ],
         cost_estimate=pl.CostEstimate(
@@ -248,7 +273,7 @@
     xs = rows[:, :lw]
     cs = rows[:, lw : 2 * lw]
     hi = rows[:, 2 * lw : 2 * lw + EXPERTS]
-    lo = rows[:, 2 * lw + EXPERTS :]
+    hi_lo = rows[:, 2 * lw :]
     w_near, w_far = exchange_weights(w_gate, w_up, w_down, y, c)
 
     def partial_sums(w):
@@ -263,7 +288,7 @@
     onehot = (
         neuron_expert[:, None] == lax.broadcasted_iota(jnp.int32, (nl, EXPERTS), 1)
     ).astype(BF)
-    scale = mm(onehot, hi, ((1,), (1,))) + mm(onehot, lo, ((1,), (1,)))
+    scale = mm(jnp.concatenate([onehot, onehot], 1), hi_lo, ((1,), (1,)))
     sig = jax.nn.sigmoid(gate)
     silu = gate * sig
     hidden = silu * upper
@@ -302,8 +327,7 @@
         1,
     ).astype(BF)
     select_common = mm(to_common, select, ((0,), (0,))).astype(BF)
-    after_coefs = near_coefs[1, 0, 0].astype(F32) * 0.0
-    chosen_rows = (mm(select, rows[:, : 2 * lw], ((0,), (0,))) + after_coefs).astype(BF)
+    chosen_rows = mm(select, rows[:, : 2 * lw], ((0,), (0,))).astype(BF)
     near_rows, far_rows = gather_rows(chosen_rows)
 
     owner = neuron_expert // E_DEV
@@ -311,15 +335,13 @@
     col_i = lax.broadcasted_iota(jnp.int32, (nl, nl), 1)
     before = jnp.sum(((owner[:, None] == owner[None, :]) & (col_i < row_i)).astype(jnp.int32), 1)
     target = owner * PEER + before
-    packing = (
-        target[None, :] == lax.broadcasted_iota(jnp.int32, (n_ep * PEER, nl), 0)
-    ).astype(BF)
+    packing = (target[None, :] == lax.broadcasted_iota(jnp.int32, (n_ep * PEER, nl), 0)).astype(BF)
     label = (neuron_expert % E_DEV * CAPN + neuron_slot + 1).astype(BF)
     common = mm(coefs, to_common, ((1,), (0,))).astype(BF)
-    packed = [mm(packing, common[i * nl : (i + 1) * nl], ((1,), (0,))).astype(BF) for i in range(3)]
     tag = jnp.broadcast_to(label[:, None], (nl, 128))
-    packed.append(mm(packing, tag, ((1,), (0,))).astype(BF))
-    sent = jnp.concatenate(packed, 1).reshape(n_ep, PEER, -1)
+    wide = [common[i * nl : (i + 1) * nl] for i in range(3)] + [tag]
+    sent = mm(packing, jnp.concatenate(wide, 1), ((1,), (0,))).astype(BF)
+    sent = sent.reshape(n_ep, PEER, -1)
     got = lax.all_to_all(sent, "ep", split_axis=0, concat_axis=0, tiled=True)
     got = got.reshape(n_ep * PEER, -1)
     turns = jnp.arange(8, dtype=jnp.int32)

time: 171 us -> 160 us (0.936)
  the two profiles are of different devices: /device:TPU:2 before, /device:TPU:1 now
where the time goes in v1:
time: 160 us
  starting transfers between devices  64.4 us (40%)
  waiting for transfers between devices  54.1 us (34%)
  local copies, waits for them, and re-layouts  13.7 us (9%)
  Pallas kernels  10.1 us (6%)
  other arithmetic  8.35 us (5%)
  matrix products  7.92 us (5%)
    ppermute x13, waiting for transfers between devices, move_y(): return lax.ppermute(v, 'tp', pairs)  29.4 us
    ppermute x8, starting transfers between devices, move_z(): return lax.ppermute(v, 'ep', pairs)  18.7 us
    ppermute x13, starting transfers between devices, move_y(): return lax.ppermute(v, 'tp', pairs)  16.8 us
    ppermute x8, waiting for transfers between devices, move_z(): return lax.ppermute(v, 'ep', pairs)  13 us
    ppermute x8, starting transfers between devices, swap_core(): return lax.ppermute(v, 'tp', [(i, i ^ 1) for i in range(2 * NY)])  11.1 us
    ppermute x6, starting transfers between devices, move_x(): return lax.ppermute(v, 'ep', pairs)  8.34 us
    ppermute x6, waiting for transfers between devices, move_x(): return lax.ppermute(v, 'ep', pairs)  8.06 us
    dot_general x12, matrix products, mm(): return lax.dot_general(a, b, (dims, ((), ())), preferred_element_type=F32)  7.92 us
  transfers between devices with their start and end apart: 37, of which 14 were waited for; matrix products, arithmetic and copies ran while one was open for 13% of the time, Pallas kernels for 6%

profile of v1, /device:TPU:1, one launch (start us, length us, event | category | flops | bytes accessed | tf_op | source)
XLA Modules:
  0.0 159.8 jit_solution(10333228321100384989)
XLA Ops:
  5.3 2.5 %collective-permute-start.4 = (bf16[16,2176]{1,0:T(8,128)(2,1)S(1)}, bf16[16,2176]{1,0:T(8,128)(2,1)S(1)}, u32[]{:S(2)}, u32[]{:S(2)}) collective-permute-start(bf16[16,2176]{1,0:T(8,128)(2,1)S(1)} %concatenate.50), channel_id=1, source_target_pairs={{0,2},{1,3},{2,0},{3,1},{4,6},{5,7},{6,4},{7,5},{8,10},{9,11},{10,... | collective-permute-start | bytes 208904 | tf_op jit(solution)/shard_map/ppermute | solution.py:23
  10.6 3.0 %collective-permute-start.1 = (bf16[168,2048]{1,0:T(8,128)(2,1)S(1)}, bf16[168,2048]{1,0:T(8,128)(2,1)S(1)}, u32[]{:S(2)}, u32[]{:S(2)}) collective-permute-start(bf16[168,2048]{1,0:T(8,128)(2,1)S(1)} %pad_maximum_fusion.5), channel_id=1, source_target_pairs={{0,128},{32,160},{64,192},{96,224},{128,0},{160,32},{192,64},{224,... | collective-permute-start | bytes 2064392 | tf_op jit(solution)/shard_map/ppermute | solution.py:33
  19.5 5.7 %collective-permute-start.6 = (bf16[4,16,2176]{2,1,0:T(8,128)(2,1)S(1)}, bf16[4,16,2176]{2,1,0:T(8,128)(2,1)S(1)}, u32[]{:S(2)}, u32[]{:S(2)}) collective-permute-start(bf16[4,16,2176]{2,1,0:T(8,128)(2,1)S(1)} %pad_maximum_fusion.8), channel_id=1, source_target_pairs={{0,28},{1,29},{2,30},{3,31},{4,0},{5,1},{6,2},{7,3},{8,4},{9,5},{1... | collective-permute-start | bytes 835592 | tf_op jit(solution)/shard_map/ppermute | solution.py:28
  25.2 3.5 %collective-permute-done.6 = bf16[4,16,2176]{2,1,0:T(8,128)(2,1)S(1)} collective-permute-done((bf16[4,16,2176]{2,1,0:T(8,128)(2,1)S(1)}, bf16[4,16,2176]{2,1,0:T(8,128)(2,1)S(1)}, u32[]{:S(2)}, u32[]{:S(2)}) %collective-permute-start.6) | collective-permute-done | bytes 278560 | tf_op jit(solution)/shard_map/ppermute | solution.py:28
  28.6 3.6 %collective-permute-start.7 = (bf16[4,16,2176]{2,1,0:T(8,128)(2,1)S(1)}, bf16[4,16,2176]{2,1,0:T(8,128)(2,1)S(1)}, u32[]{:S(2)}, u32[]{:S(2)}) collective-permute-start(bf16[4,16,2176]{2,1,0:T(8,128)(2,1)S(1)} %collective-permute-done.6), channel_id=1, source_target_pairs={{0,28},{1,29},{2,30},{3,31},{4,0},{5,1},{6,2},{7,3},{8,4},{9,5},{1... | collective-permute-start | bytes 835592 | tf_op jit(solution)/shard_map/ppermute | solution.py:28
  32.2 3.5 %collective-permute-done.7 = bf16[4,16,2176]{2,1,0:T(8,128)(2,1)S(1)} collective-permute-done((bf16[4,16,2176]{2,1,0:T(8,128)(2,1)S(1)}, bf16[4,16,2176]{2,1,0:T(8,128)(2,1)S(1)}, u32[]{:S(2)}, u32[]{:S(2)}) %collective-permute-start.7) | collective-permute-done | bytes 278560 | tf_op jit(solution)/shard_map/ppermute | solution.py:28
  35.7 3.5 %collective-permute-start.8 = (bf16[4,16,2176]{2,1,0:T(8,128)(2,1)S(1)}, bf16[4,16,2176]{2,1,0:T(8,128)(2,1)S(1)}, u32[]{:S(2)}, u32[]{:S(2)}) collective-permute-start(bf16[4,16,2176]{2,1,0:T(8,128)(2,1)S(1)} %collective-permute-done.7), channel_id=1, source_target_pairs={{0,28},{1,29},{2,30},{3,31},{4,0},{5,1},{6,2},{7,3},{8,4},{9,5},{1... | collective-permute-start | bytes 835592 | tf_op jit(solution)/shard_map/ppermute | solution.py:28
  39.3 5.0 %collective-permute-done.2 = bf16[168,2048]{1,0:T(8,128)(2,1)} collective-permute-done((bf16[168,2048]{1,0:T(8,128)(2,1)}, bf16[168,2048]{1,0:T(8,128)(2,1)}, u32[]{:S(2)}, u32[]{:S(2)}) %collective-permute-start.2) | collective-permute-done | bytes 688160 | tf_op jit(solution)/shard_map/ppermute | solution.py:33
  46.4 5.7 %collective-permute-start.9 = (bf16[2,16,2176]{2,1,0:T(8,128)(2,1)S(1)}, bf16[2,16,2176]{2,1,0:T(8,128)(2,1)S(1)}, u32[]{:S(2)}, u32[]{:S(2)}) collective-permute-start(bf16[2,16,2176]{2,1,0:T(8,128)(2,1)S(1)} %slice.126), channel_id=1, source_target_pairs={{0,28},{1,29},{2,30},{3,31},{4,0},{5,1},{6,2},{7,3},{8,4},{9,5},{1... | collective-permute-start | bytes 417800 | tf_op jit(solution)/shard_map/ppermute | solution.py:28
  52.3 2.7 %collective-permute-done.9 = bf16[2,16,2176]{2,1,0:T(8,128)(2,1)S(1)} collective-permute-done((bf16[2,16,2176]{2,1,0:T(8,128)(2,1)S(1)}, bf16[2,16,2176]{2,1,0:T(8,128)(2,1)S(1)}, u32[]{:S(2)}, u32[]{:S(2)}) %collective-permute-start.9) | collective-permute-done | bytes 139296 | tf_op jit(solution)/shard_map/ppermute | solution.py:28
  55.0 3.4 %collective-permute-done.13 = bf16[2,16,2176]{2,1,0:T(8,128)(2,1)S(1)} collective-permute-done((bf16[2,16,2176]{2,1,0:T(8,128)(2,1)S(1)}, bf16[2,16,2176]{2,1,0:T(8,128)(2,1)S(1)}, u32[]{:S(2)}, u32[]{:S(2)}) %collective-permute-start.13) | collective-permute-done | bytes 139296 | tf_op jit(solution)/shard_map/ppermute | solution.py:28
  70.2 4.2 %collective-permute-done.17 = bf16[168,512]{1,0:T(8,128)(2,1)S(1)} collective-permute-done((bf16[168,512]{1,0:T(8,128)(2,1)S(1)}, bf16[168,512]{1,0:T(8,128)(2,1)S(1)}, u32[]{:S(2)}, u32[]{:S(2)}) %collective-permute-start.17) | collective-permute-done | bytes 172064 | tf_op jit(solution)/shard_map/ppermute | solution.py:33
  78.5 4.5 %collective-permute-done.20 = bf16[232,512]{1,0:T(8,128)(2,1)S(1)} collective-permute-done((bf16[232,512]{1,0:T(8,128)(2,1)S(1)}, bf16[232,512]{1,0:T(8,128)(2,1)S(1)}, u32[]{:S(2)}, u32[]{:S(2)}) %collective-permute-start.20) | collective-permute-done | bytes 237600 | tf_op jit(solution)/shard_map/ppermute | solution.py:33
  83.0 4.8 %collective-permute-done.19 = bf16[232,512]{1,0:T(8,128)(2,1)S(1)} collective-permute-done((bf16[232,512]{1,0:T(8,128)(2,1)S(1)}, bf16[232,512]{1,0:T(8,128)(2,1)S(1)}, u32[]{:S(2)}, u32[]{:S(2)}) %collective-permute-start.19) | collective-permute-done | bytes 237600 | tf_op jit(solution)/shard_map/ppermute | solution.py:33
  94.1 3.7 %shard_map.136 = (bf16[8,16,2176]{2,1,0:T(8,128)(2,1)S(1)}, bf16[8,16,2176]{2,1,0:T(8,128)(2,1)}, bf16[8,16,2176]{2,1,0:T(8,128)(2,1)}, bf16[8,16,2176]{2,1,0:T(8,128)(2,1)}) custom-call(s32[8]{0:T(128)S(1)} %and_select_fusion.6.order, bf16[4,232,512]{2,1,0:T(8,128)(2,1)S(1)} %pad_maximum_fusion.2.near, ...), custom_call_target="tpu_custom_call" | custom-call | flops 1409286144 | bytes 8388608 | tf_op jit(solution)/shard_map/pallas_call | solution.py:121
  104.5 5.2 %all-to-all-start.1 = ((bf16[32,4,1664]{2,1,0:T(4,128)(2,1)}), bf16[32,4,1664]{2,1,0:T(4,128)(2,1)}, u32[]{:S(2)}, u32[]{:S(2)}) async-start(bf16[32,4,1664]{2,1,0:T(4,128)(2,1)} %reshape.49), calls=%async_computation.1 | async-start | bytes 851968 | tf_op jit(solution)/shard_map/all_to_all | solution.py:345
  109.7 7.7 %collective-permute-done.28.refs_4_ = bf16[256,2048]{1,0:T(8,128)(2,1)S(1)} collective-permute-done((bf16[256,2048]{1,0:T(8,128)(2,1)S(1)}, bf16[256,2048]{1,0:T(8,128)(2,1)S(1)}, u32[]{:S(2)}, u32[]{:S(2)}) %collective-permute-start.28) | collective-permute-done | bytes 1048608 | tf_op jit(solution)/shard_map/ppermute | solution.py:33
  119.9 8.0 %collective-permute-done.23 = bf16[8,16,2176]{2,1,0:T(8,128)(2,1)} collective-permute-done((bf16[8,16,2176]{2,1,0:T(8,128)(2,1)}, bf16[8,16,2176]{2,1,0:T(8,128)(2,1)}, u32[]{:S(2)}, u32[]{:S(2)}) %collective-permute-start.23) | collective-permute-done | bytes 557088 | tf_op jit(solution)/shard_map/ppermute | solution.py:23
  128.6 3.1 %collective-permute-start.34 = (bf16[256,2048]{1,0:T(8,128)(2,1)S(1)}, bf16[256,2048]{1,0:T(8,128)(2,1)}, u32[]{:S(2)}, u32[]{:S(2)}) collective-permute-start(bf16[256,2048]{1,0:T(8,128)(2,1)S(1)} %collective-permute-done.28.refs_4_), channel_id=1, source_target_pairs={{0,32},{32,0},{64,96},{96,64},{128,160},{160,128},{192,224},{224,1... | collective-permute-start | bytes 3145736 | tf_op jit(solution)/shard_map/ppermute | solution.py:37
  131.8 2.5 %add_convert_fusion = bf16[8,16,2176]{2,1,0:T(8,128)(2,1)} fusion(bf16[8,16,2176]{2,1,0:T(8,128)(2,1)} %collective-permute-done.25, bf16[8,16,2176]{2,1,0:T(8,128)(2,1)} %collective-permute-done.24, bf16[8,16,2176]{2,1,0:T(8,128)(2,1)} %collective-permute-done.23, bf16[8,16,2176]{2,1,0:T(8,128)(2,1)S(1)} %copy-done.2), kind=kLoop, calls=%fused_computation.23 | loop fusion | flops 2228224 | bytes 2785280 | tf_op jit(solution)/shard_map/convert_element_type | solution.py:141
  134.3 4.2 %all-to-all-start = ((bf16[8,16,2176]{2,1,0:T(8,128)(2,1)}), bf16[8,16,2176]{2,1,0:T(8,128)(2,1)}, u32[]{:S(2)}, u32[]{:S(2)}) async-start(bf16[8,16,2176]{2,1,0:T(8,128)(2,1)} %add_convert_fusion), calls=%async_computation | async-start | bytes 1114112 | tf_op jit(solution)/shard_map/all_to_all | solution.py:143
  139.0 3.6 %collective-permute-start.32 = (bf16[128,2048]{1,0:T(8,128)(2,1)}, bf16[128,2048]{1,0:T(8,128)(2,1)}, u32[]{:S(2)}, u32[]{:S(2)}) collective-permute-start(bf16[128,2048]{1,0:T(8,128)(2,1)} %collective-permute-done.27.refs_2_), channel_id=1, source_target_pairs={{0,32},{32,0},{64,96},{96,64},{128,160},{160,128},{192,224},{224,1... | collective-permute-start | bytes 1572872 | tf_op jit(solution)/shard_map/ppermute | solution.py:37
  147.6 6.4 %shard_map.137 = (bf16[2,64,8192]{2,1,0:T(8,128)(2,1)}, bf16[2,64,8192]{2,1,0:T(8,128)(2,1)}, bf16[2,64,8192]{2,1,0:T(8,128)(2,1)}) custom-call(s32[8]{0:T(128)S(1)} %fusion.53.cols, bf16[128,1664]{1,0:T(8,128)(2,1)S(1)} %copy-done, bf16[512,256]{1,0:T(8,128)(2,1)S(1)} %convolution_convert_fusion.3.select, ...), custom_call_target="tpu_custom_call" | custom-call | flops 805306368 | bytes 16777216 | tf_op jit(solution)/shard_map/pallas_call | solution.py:215
  154.0 3.2 %all-to-all-done = bf16[8,16,2176]{2,1,0:T(8,128)(2,1)} async-done(((bf16[8,16,2176]{2,1,0:T(8,128)(2,1)}), bf16[8,16,2176]{2,1,0:T(8,128)(2,1)}, u32[]{:S(2)}, u32[]{:S(2)}) %all-to-all-start) | async-done | bytes 557088 | tf_op jit(solution)/shard_map/all_to_all | solution.py:143
  (163 shorter events, 55.4 us)
Async XLA Ops:
  3.3 13.8 %collective-permute-start.5 = (bf16[16,2176]{1,0:T(8,128)(2,1)S(1)}, bf16[16,2176]{1,0:T(8,128)(2,1)S(1)}, u32[]{:S(2)}, u32[]{:S(2)}) collective-permute-start(bf16[16,2176]{1,0:T(8,128)(2,1)S(1)} %concatenate.50), channel_id=1, source_target_pairs={{0,1},{1,2},{2,3},{3,0},{4,5},{5,6},{6,7},{7,4},{8,9},{9,10},{10,1... | collective-permute-start | bytes 208904 | tf_op jit(solution)/shard_map/ppermute | solution.py:23
  5.3 14.1 %collective-permute-start.4 = (bf16[16,2176]{1,0:T(8,128)(2,1)S(1)}, bf16[16,2176]{1,0:T(8,128)(2,1)S(1)}, u32[]{:S(2)}, u32[]{:S(2)}) collective-permute-start(bf16[16,2176]{1,0:T(8,128)(2,1)S(1)} %concatenate.50), channel_id=1, source_target_pairs={{0,2},{1,3},{2,0},{3,1},{4,6},{5,7},{6,4},{7,5},{8,10},{9,11},{10,... | collective-permute-start | bytes 208904 | tf_op jit(solution)/shard_map/ppermute | solution.py:23
  7.8 11.6 %collective-permute-start.3 = (bf16[16,2176]{1,0:T(8,128)(2,1)S(1)}, bf16[16,2176]{1,0:T(8,128)(2,1)S(1)}, u32[]{:S(2)}, u32[]{:S(2)}) collective-permute-start(bf16[16,2176]{1,0:T(8,128)(2,1)S(1)} %concatenate.50), channel_id=1, source_target_pairs={{0,3},{1,0},{2,1},{3,2},{4,7},{5,4},{6,5},{7,6},{8,11},{9,8},{10,9... | collective-permute-start | bytes 208904 | tf_op jit(solution)/shard_map/ppermute | solution.py:23
  10.6 28.7 %collective-permute-start.1 = (bf16[168,2048]{1,0:T(8,128)(2,1)S(1)}, bf16[168,2048]{1,0:T(8,128)(2,1)S(1)}, u32[]{:S(2)}, u32[]{:S(2)}) collective-permute-start(bf16[168,2048]{1,0:T(8,128)(2,1)S(1)} %pad_maximum_fusion.5), channel_id=1, source_target_pairs={{0,128},{32,160},{64,192},{96,224},{128,0},{160,32},{192,64},{224,... | collective-permute-start | bytes 2064392 | tf_op jit(solution)/shard_map/ppermute | solution.py:33
  14.5 29.9 %collective-permute-start.2 = (bf16[168,2048]{1,0:T(8,128)(2,1)}, bf16[168,2048]{1,0:T(8,128)(2,1)}, u32[]{:S(2)}, u32[]{:S(2)}) collective-permute-start(bf16[168,2048]{1,0:T(8,128)(2,1)} %pad_maximum_fusion.6), channel_id=1, source_target_pairs={{0,64},{32,96},{64,128},{96,160},{128,192},{160,224},{192,0},{224,... | collective-permute-start | bytes 2064392 | tf_op jit(solution)/shard_map/ppermute | solution.py:33
  17.1 28.4 %collective-permute-start = (bf16[168,2048]{1,0:T(8,128)(2,1)S(1)}, bf16[168,2048]{1,0:T(8,128)(2,1)S(1)}, u32[]{:S(2)}, u32[]{:S(2)}) collective-permute-start(bf16[168,2048]{1,0:T(8,128)(2,1)S(1)} %pad_maximum_fusion.4), channel_id=1, source_target_pairs={{0,192},{32,224},{64,0},{96,32},{128,64},{160,96},{192,128},{224,1... | collective-permute-start | bytes 2064392 | tf_op jit(solution)/shard_map/ppermute | solution.py:33
  19.5 9.1 %collective-permute-start.6 = (bf16[4,16,2176]{2,1,0:T(8,128)(2,1)S(1)}, bf16[4,16,2176]{2,1,0:T(8,128)(2,1)S(1)}, u32[]{:S(2)}, u32[]{:S(2)}) collective-permute-start(bf16[4,16,2176]{2,1,0:T(8,128)(2,1)S(1)} %pad_maximum_fusion.8), channel_id=1, source_target_pairs={{0,28},{1,29},{2,30},{3,31},{4,0},{5,1},{6,2},{7,3},{8,4},{9,5},{1... | collective-permute-start | bytes 835592 | tf_op jit(solution)/shard_map/ppermute | solution.py:28
  35.7 10.6 %collective-permute-start.8 = (bf16[4,16,2176]{2,1,0:T(8,128)(2,1)S(1)}, bf16[4,16,2176]{2,1,0:T(8,128)(2,1)S(1)}, u32[]{:S(2)}, u32[]{:S(2)}) collective-permute-start(bf16[4,16,2176]{2,1,0:T(8,128)(2,1)S(1)} %collective-permute-done.7), channel_id=1, source_target_pairs={{0,28},{1,29},{2,30},{3,31},{4,0},{5,1},{6,2},{7,3},{8,4},{9,5},{1... | collective-permute-start | bytes 835592 | tf_op jit(solution)/shard_map/ppermute | solution.py:28
  39.2 12.8 %collective-permute-start.12 = (bf16[4,16,2176]{2,1,0:T(8,128)(2,1)S(1)}, bf16[4,16,2176]{2,1,0:T(8,128)(2,1)S(1)}, u32[]{:S(2)}, u32[]{:S(2)}) collective-permute-start(bf16[4,16,2176]{2,1,0:T(8,128)(2,1)S(1)} %collective-permute-done.11), channel_id=1, source_target_pairs={{0,4},{1,5},{2,6},{3,7},{4,8},{5,9},{6,10},{7,11},{8,12},{9,13},{1... | collective-permute-start | bytes 835592 | tf_op jit(solution)/shard_map/ppermute | solution.py:28
  45.8 13.0 %collective-permute-start.14 = (bf16[4,168,1024]{2,1,0:T(8,128)(2,1)S(1)}, bf16[4,168,1024]{2,1,0:T(8,128)(2,1)S(1)}, u32[]{:S(2)}, u32[]{:S(2)}) collective-permute-start(bf16[4,168,1024]{2,1,0:T(8,128)(2,1)S(1)} %pad_maximum_fusion.1), channel_id=1, source_target_pairs={{0,32},{32,0},{64,96},{96,64},{128,160},{160,128},{192,224},{224,1... | collective-permute-start | bytes 4128776 | tf_op jit(solution)/shard_map/ppermute | solution.py:37
  76.4 11.4 %collective-permute-start.19 = (bf16[232,512]{1,0:T(8,128)(2,1)S(1)}, bf16[232,512]{1,0:T(8,128)(2,1)S(1)}, u32[]{:S(2)}, u32[]{:S(2)}) collective-permute-start(bf16[232,512]{1,0:T(8,128)(2,1)S(1)} %get-tuple-element.59), channel_id=1, source_target_pairs={{0,192},{32,224},{64,0},{96,32},{128,64},{160,96},{192,128},{224,1... | collective-permute-start | bytes 712712 | tf_op jit(solution)/shard_map/ppermute | solution.py:33
  78.2 10.5 %collective-permute-start.21 = (bf16[232,512]{1,0:T(8,128)(2,1)S(1)}, bf16[232,512]{1,0:T(8,128)(2,1)S(1)}, u32[]{:S(2)}, u32[]{:S(2)}) collective-permute-start(bf16[232,512]{1,0:T(8,128)(2,1)S(1)} %get-tuple-element.59), channel_id=1, source_target_pairs={{0,64},{32,96},{64,128},{96,160},{128,192},{160,224},{192,0},{224,... | collective-permute-start | bytes 712712 | tf_op jit(solution)/shard_map/ppermute | solution.py:33
  91.3 26.1 %collective-permute-start.28 = (bf16[256,2048]{1,0:T(8,128)(2,1)S(1)}, bf16[256,2048]{1,0:T(8,128)(2,1)S(1)}, u32[]{:S(2)}, u32[]{:S(2)}) collective-permute-start(bf16[256,2048]{1,0:T(8,128)(2,1)S(1)} %convolution_convert_fusion.refs_0_), channel_id=1, source_target_pairs={{0,64},{32,96},{64,128},{96,160},{128,192},{160,224},{192,0},{224,... | collective-permute-start | bytes 3145736 | tf_op jit(solution)/shard_map/ppermute | solution.py:33
  92.1 26.9 %collective-permute-start.26 = (bf16[256,2048]{1,0:T(8,128)(2,1)S(1)}, bf16[256,2048]{1,0:T(8,128)(2,1)S(1)}, u32[]{:S(2)}, u32[]{:S(2)}) collective-permute-start(bf16[256,2048]{1,0:T(8,128)(2,1)S(1)} %convolution_convert_fusion.refs_0_), channel_id=1, source_target_pairs={{0,192},{32,224},{64,0},{96,32},{128,64},{160,96},{192,128},{224,1... | collective-permute-start | bytes 3145736 | tf_op jit(solution)/shard_map/ppermute | solution.py:33
  97.8 30.1 %collective-permute-start.23 = (bf16[8,16,2176]{2,1,0:T(8,128)(2,1)}, bf16[8,16,2176]{2,1,0:T(8,128)(2,1)}, u32[]{:S(2)}, u32[]{:S(2)}) collective-permute-start(bf16[8,16,2176]{2,1,0:T(8,128)(2,1)} %get-tuple-element.14), channel_id=1, source_target_pairs={{0,1},{1,2},{2,3},{3,0},{4,5},{5,6},{6,7},{7,4},{8,9},{9,10},{10,1... | collective-permute-start | bytes 1671176 | tf_op jit(solution)/shard_map/ppermute | solution.py:23
  98.1 30.4 %collective-permute-start.24 = (bf16[8,16,2176]{2,1,0:T(8,128)(2,1)}, bf16[8,16,2176]{2,1,0:T(8,128)(2,1)}, u32[]{:S(2)}, u32[]{:S(2)}) collective-permute-start(bf16[8,16,2176]{2,1,0:T(8,128)(2,1)} %get-tuple-element.15), channel_id=1, source_target_pairs={{0,2},{1,3},{2,0},{3,1},{4,6},{5,7},{6,4},{7,5},{8,10},{9,11},{10,... | collective-permute-start | bytes 1671176 | tf_op jit(solution)/shard_map/ppermute | solution.py:23
  99.0 32.7 %collective-permute-start.25 = (bf16[8,16,2176]{2,1,0:T(8,128)(2,1)}, bf16[8,16,2176]{2,1,0:T(8,128)(2,1)}, u32[]{:S(2)}, u32[]{:S(2)}) collective-permute-start(bf16[8,16,2176]{2,1,0:T(8,128)(2,1)} %get-tuple-element.16), channel_id=1, source_target_pairs={{0,3},{1,0},{2,1},{3,2},{4,7},{5,4},{6,5},{7,6},{8,11},{9,8},{10,9... | collective-permute-start | bytes 1671176 | tf_op jit(solution)/shard_map/ppermute | solution.py:23
  104.5 29.8 %all-to-all-start.1 = ((bf16[32,4,1664]{2,1,0:T(4,128)(2,1)}), bf16[32,4,1664]{2,1,0:T(4,128)(2,1)}, u32[]{:S(2)}, u32[]{:S(2)}) async-start(bf16[32,4,1664]{2,1,0:T(4,128)(2,1)} %reshape.49), calls=%async_computation.1 | async-start | bytes 851968 | tf_op jit(solution)/shard_map/all_to_all | solution.py:345
  117.4 29.1 %collective-permute-start.30 = (bf16[256,2048]{1,0:T(8,128)(2,1)S(1)}, bf16[256,2048]{1,0:T(8,128)(2,1)}, u32[]{:S(2)}, u32[]{:S(2)}) collective-permute-start(bf16[256,2048]{1,0:T(8,128)(2,1)S(1)} %convolution_convert_fusion.refs_0_), channel_id=1, source_target_pairs={{0,32},{32,0},{64,96},{96,64},{128,160},{160,128},{192,224},{224,1... | collective-permute-start | bytes 3145736 | tf_op jit(solution)/shard_map/ppermute | solution.py:37
  119.1 19.4 %collective-permute-start.29 = (bf16[128,2048]{1,0:T(8,128)(2,1)}, bf16[128,2048]{1,0:T(8,128)(2,1)}, u32[]{:S(2)}, u32[]{:S(2)}) collective-permute-start(bf16[128,2048]{1,0:T(8,128)(2,1)} %slice.154), channel_id=1, source_target_pairs={{0,64},{32,96},{64,128},{96,160},{128,192},{160,224},{192,0},{224,... | collective-permute-start | bytes 1572872 | tf_op jit(solution)/shard_map/ppermute | solution.py:33
  127.9 11.1 %collective-permute-start.27 = (bf16[128,2048]{1,0:T(8,128)(2,1)}, bf16[128,2048]{1,0:T(8,128)(2,1)}, u32[]{:S(2)}, u32[]{:S(2)}) collective-permute-start(bf16[128,2048]{1,0:T(8,128)(2,1)} %slice.153), channel_id=1, source_target_pairs={{0,192},{32,224},{64,0},{96,32},{128,64},{160,96},{192,128},{224,1... | collective-permute-start | bytes 1572872 | tf_op jit(solution)/shard_map/ppermute | solution.py:33
  128.6 18.0 %collective-permute-start.34 = (bf16[256,2048]{1,0:T(8,128)(2,1)S(1)}, bf16[256,2048]{1,0:T(8,128)(2,1)}, u32[]{:S(2)}, u32[]{:S(2)}) collective-permute-start(bf16[256,2048]{1,0:T(8,128)(2,1)S(1)} %collective-permute-done.28.refs_4_), channel_id=1, source_target_pairs={{0,32},{32,0},{64,96},{96,64},{128,160},{160,128},{192,224},{224,1... | collective-permute-start | bytes 3145736 | tf_op jit(solution)/shard_map/ppermute | solution.py:37
  131.7 14.9 %collective-permute-start.31 = (bf16[256,2048]{1,0:T(8,128)(2,1)S(1)}, bf16[256,2048]{1,0:T(8,128)(2,1)}, u32[]{:S(2)}, u32[]{:S(2)}) collective-permute-start(bf16[256,2048]{1,0:T(8,128)(2,1)S(1)} %collective-permute-done.26.refs_1_), channel_id=1, source_target_pairs={{0,32},{32,0},{64,96},{96,64},{128,160},{160,128},{192,224},{224,1... | collective-permute-start | bytes 3145736 | tf_op jit(solution)/shard_map/ppermute | solution.py:37
  134.3 22.9 %all-to-all-start = ((bf16[8,16,2176]{2,1,0:T(8,128)(2,1)}), bf16[8,16,2176]{2,1,0:T(8,128)(2,1)}, u32[]{:S(2)}, u32[]{:S(2)}) async-start(bf16[8,16,2176]{2,1,0:T(8,128)(2,1)} %add_convert_fusion), calls=%async_computation | async-start | bytes 1114112 | tf_op jit(solution)/shard_map/all_to_all | solution.py:143
  (30 other events, 678.6 us)
